TPU v7x, 256 devices: a whole 4x4x8 slice. The times are simulated.
256 devices in a mesh: row: 32 (over z, y), col: 8 (over x, core).
Axes of the slice: x: 4, y: 4, z: 8, core: 2. Of those that a mesh axis runs over, the one named last changes fastest.
Arguments:
- feats: bfloat16 [131072, 256], P(('row', 'col')), may hold values from -6 to 6
- w_msg: bfloat16 [256, 256], replicated, may hold values from -0.375 to 0.375
- w_self: bfloat16 [256, 256], replicated, may hold values from -0.375 to 0.375
- bias: float32 [256], replicated, may hold values from -3 to 3
- hit_mask: int32 [131072], P(('row', 'col')), may hold values 0 or 1
- block_cols: int32 [32, 8, 96], P('row', 'col'), may hold values from 0 to 127, as said below
- block_count: int32 [32, 8], P('row', 'col'), may hold values from 32 to 96, as said below
- edge_vals: bfloat16 [32, 8, 96, 128, 128], P('row', 'col'), may hold values from -0.125 to 0.125
- grad_out: bfloat16 [131072, 256], P(('row', 'col')), may hold values from -3 to 3
Outputs:
- hidden: bfloat16 [131072, 256], P(('row', 'col'))
- grad_feats: bfloat16 [131072, 256], P(('row', 'col'))
- edge_grad: bfloat16 [32, 8, 96, 128, 128], P('row', 'col')
- w_msg_grad: float32 [256, 256], replicated
- w_self_grad: float32 [256, 256], replicated
- bias_grad: float32 [256], replicated
Inputs may be any that keep to these rules, and one draw needn't show every extreme that they name: `block_cols`: slot s of a tile serves the tile's local block row s % 32; the block columns of the slots that serve one block row of one tile are different. Slots from block_count on are unused.
All inputs are finite; a program needn't handle non-finite values. No bound on the sum of `hit_mask` on one device may be relied on, other than what follows from the above.
Results may differ from a plain program's by a relative error of at most 0.015.
Values may be sent and summed in bfloat16 or wider, within the bound.
A program may use at most 128 MiB of HBM per device.

v0:
```python
import math
import jax
import jax.numpy as jnp
from jax import lax
from jax.sharding import PartitionSpec as P


def activate(pre, row_mask, grad_in):
    sig = jax.nn.sigmoid(pre)
    hidden = (pre * sig * row_mask).astype(jnp.bfloat16)
    deriv = sig * (1.0 + pre * (1.0 - sig))
    grad_pre = (grad_in.astype(jnp.float32) * row_mask * deriv).astype(jnp.bfloat16)
    return (hidden, grad_pre)


def per_device(feats, w_msg, w_self, bias, hit_mask, block_cols, block_count, edge_vals, grad_out):
    row_count = lax.axis_size("row")
    col_count = lax.axis_size("col")
    own_rows = feats.shape[0]
    width = feats.shape[1]
    row_mask = hit_mask.astype(jnp.float32)[:, None]
    messages = (jnp.dot(feats, w_msg, preferred_element_type=jnp.float32) * row_mask).astype(
        jnp.bfloat16
    )
    column_msgs = lax.all_gather(messages, "row", axis=0, tiled=True)
    slot_cols = block_cols[0, 0]
    edge_block = edge_vals[0, 0]
    slot_total = edge_block.shape[0]
    edge_size = edge_block.shape[1]
    tile_rows = col_count * own_rows // edge_size
    tile_cols = row_count * own_rows // edge_size
    slot_depth = slot_total // tile_rows
    slot_flags = jnp.arange(slot_total, dtype=jnp.int32) < block_count[0, 0]
    edge_live = (edge_block * slot_flags.astype(jnp.bfloat16)[:, None, None]).reshape(
        slot_depth, tile_rows, edge_size, edge_size
    )
    col_blocks = column_msgs.reshape(tile_cols, edge_size, width)[slot_cols].reshape(
        slot_depth, tile_rows, edge_size, width
    )
    partial_value = jnp.einsum(
        "krij,krjf->rif", edge_live, col_blocks, preferred_element_type=jnp.float32
    ).reshape(tile_rows * edge_size, width)
    summed = lax.psum_scatter(
        partial_value.astype(jnp.bfloat16), "col", scatter_dimension=0, tiled=True
    ).astype(jnp.float32)
    pre = summed + jnp.dot(feats, w_self, preferred_element_type=jnp.float32) + bias
    hidden, grad_pre = activate(pre, row_mask, grad_out)
    grad_rows_all = lax.all_gather(grad_pre, "col", axis=0, tiled=True)
    grad_tile = grad_rows_all.reshape(tile_rows, edge_size, width)
    backward = jnp.einsum(
        "krij,rif->krjf", edge_live, grad_tile, preferred_element_type=jnp.float32
    ).reshape(slot_total, edge_size, width)
    back_part = jax.ops.segment_sum(backward, slot_cols, num_segments=tile_cols).reshape(
        tile_cols * edge_size, width
    )
    edge_grad = (
        jnp.einsum(
            "rif,krjf->krij", grad_tile, col_blocks, preferred_element_type=jnp.float32
        ).reshape(slot_total, edge_size, edge_size)
        * slot_flags.astype(jnp.float32)[:, None, None]
    ).astype(jnp.bfloat16)
    grad_sum = lax.psum_scatter(
        back_part.astype(jnp.bfloat16), "row", scatter_dimension=0, tiled=True
    ).astype(jnp.float32)
    grad_msg = (grad_sum * row_mask).astype(jnp.bfloat16)
    grad_feats = (
        jnp.einsum("hg,fg->hf", grad_msg, w_msg, preferred_element_type=jnp.float32)
        + jnp.einsum("hg,fg->hf", grad_pre, w_self, preferred_element_type=jnp.float32)
    ).astype(jnp.bfloat16)
    local_msg = jnp.einsum("hf,hg->fg", feats, grad_msg, preferred_element_type=jnp.float32)
    local_self = jnp.einsum("hf,hg->fg", feats, grad_pre, preferred_element_type=jnp.float32)
    local_bias = jnp.sum(grad_pre.astype(jnp.float32), axis=0)
    total_msg, total_self, total_bias = lax.psum(
        (local_msg, local_self, local_bias), ("row", "col")
    )
    factor = 1.0 / math.sqrt(own_rows * row_count * col_count)
    return (
        hidden,
        grad_feats,
        edge_grad[None, None],
        total_msg * factor,
        total_self * factor,
        total_bias * factor,
    )


def solution(mesh):
    placed = (
        P(("row", "col"), None),
        P(),
        P(),
        P(),
        P(("row", "col")),
        P("row", "col", None),
        P("row", "col"),
        P("row", "col", None, None, None),
        P(("row", "col"), None),
    )
    return jax.shard_map(
        per_device,
        mesh=mesh,
        in_specs=placed,
        out_specs=(
            P(("row", "col"), None),
            P(("row", "col"), None),
            P("row", "col", None, None, None),
            P(),
            P(),
            P(),
        ),
        check_vma=False,
    )
```

profile of v0, /device:TPU:2, one launch (start us, length us, event | category | flops | bytes accessed | tf_op | source)
XLA Modules:
  0.0 757.9 jit_solution(17679265204071514697)
XLA Ops:
  7.2 0.0 copy-start
  7.2 0.0 all-gather.3.cloned.1.call-start
  7.2 0.7 convert_element_type.67
  7.9 0.2 copy-done
  8.1 1.8 fusion.12
  10.0 0.0 all-gather.3.cloned.1.call-update
  10.0 0.0 reduce-scatter.3.cloned.1.call-start
  10.7 0.7 fusion.16
  11.4 100.7 %all-gather.3.cloned.1.call-done = bf16[16384,256]{1,0:T(8,128)(2,1)} async-done(((bf16[512,256]{1,0:T(8,128)(2,1)}), bf16[16384,256]{1,0:T(8,128)(2,1)}) %all-gather.3.cloned.1.call-update) | async-done | bytes 8388624 | tf_op jit(solution)/shard_map/all_gather | solution.py:25
  112.0 0.0 copy-start.2
  112.0 9.5 %gather_fusion = bf16[96,128,256]{2,1,0:T(8,128)(2,1)} fusion(bf16[128,128,256]{2,1,0:T(8,128)(2,1)} %bitcast.53, s32[1024]{0:T(1024)S(1)} %pad_clamp_fusion), kind=kCustom, calls=%fused_computation | custom fusion | bytes 12583296 | tf_op jit(solution)/shard_map/gather | solution.py:37
  121.5 0.0 copy-done.2
  121.5 0.0 copy-start.5
  121.5 5.5 bitcast_convert_fusion
  127.0 0.0 reduce-scatter.3.cloned.1.call-update
  127.0 0.0 all-gather.5.cloned.1.call-start
  127.1 30.4 %reduce-scatter.3.cloned.1.call-done = bf16[512,256]{1,0:T(8,128)(2,1)} async-done(((bf16[4096,256]{1,0:T(8,128)(2,1)}), bf16[512,256]{1,0:T(8,128)(2,1)}) %reduce-scatter.3.cloned.1.call-update) | async-done | bytes 262160 | tf_op jit(solution)/shard_map/reduce_scatter | solution.py:43
  157.5 0.0 copy-done.5
  157.5 2.3 convert_reduce_fusion
  159.8 0.0 all-gather.5.cloned.1.call-update
  159.8 0.0 reduce-scatter.5.cloned.1.call-start
  159.9 28.7 %all-gather.5.cloned.1.call-done = bf16[4096,256]{1,0:T(8,128)(2,1)} async-done(((bf16[512,256]{1,0:T(8,128)(2,1)}), bf16[4096,256]{1,0:T(8,128)(2,1)}) %all-gather.5.cloned.1.call-update) | async-done | bytes 2097168 | tf_op jit(solution)/shard_map/all_gather | solution.py:48
  188.6 8.0 %convolution_bitcast_fusion = f32[3,32,128,256]{2,3,0,1:T(8,128)} fusion(bf16[32,128,256,1]{2,1,3,0:T(8,128)(2,1)} %bitcast.51, bf16[3,32,128,128]{3,2,1,0:T(8,128)(2,1)S(1)} %bitcast.55, bf16[3,32]{0,1:T(8,128)(2,1)S(1)} %fusion.15), kind=kOutput, calls=%fused_computation.7 | convolution fusion | flops 811597824 | bytes 17825984 | tf_op jit(solution)/shard_map/krij,rif->krjf/dot_general | solution.py:50
  196.6 12.6 %copy.22 = f32[3,32,128,256]{3,2,1,0:T(8,128)} copy(f32[3,32,128,256]{2,3,0,1:T(8,128)} %convolution_bitcast_fusion) | data formatting | bytes 25165824 | tf_op jit(solution)/shard_map/krij,rif->krjf/transpose | solution.py:50
  209.2 0.0 copy-start.6
  209.2 7.8 %broadcast_in_dim.2 = f32[128,128,256]{2,1,0:T(8,128)} broadcast(f32[]{:T(128)} %constant.4.clone.1), dimensions={} | broadcast | bytes 16777220 | tf_op jit(solution)/shard_map/broadcast_in_dim | solution.py:53
  217.0 0.0 copy-done.6
  217.0 29.1 %scatter_fusion = f32[128,128,256]{2,1,0:T(8,128)} fusion(f32[128,128,256]{2,1,0:T(8,128)} %broadcast_in_dim.2, s32[96]{0:T(128)S(1)} %bitcast.57, f32[96,128,256]{2,1,0:T(8,128)} %bitcast.46), kind=kCustom, calls=%fused_computation.1 | custom fusion | flops 3145728 | bytes 37749120 | tf_op jit(solution)/shard_map/scatter-add | solution.py:53
  246.1 9.0 %convert_element_type.75 = bf16[128,128,256]{2,1,0:T(8,128)(2,1)} convert(f32[128,128,256]{2,1,0:T(8,128)} %scatter_fusion) | non-fusion elementwise | flops 4194304 | bytes 25165824 | tf_op jit(solution)/shard_map/convert_element_type | solution.py:63
  255.1 0.0 copy-start.3
  255.1 0.0 copy-start.1
  255.1 0.0 reduce-scatter.5.cloned.1.call-update
  255.2 0.0 all-reduce.3.cloned.1.call-start
  255.2 78.1 %psum.23 = f32[256]{0:T(256)S(1)} all-reduce(f32[256]{0:T(256)S(1)} %get-tuple-element.20), channel_id=1, replica_groups=mesh['row'=32,'col'=8] {'row','col'}, use_global_device_ids=true, to_apply=%region_6.0 | all-reduce | flops 256 | bytes 2048 | tf_op jit(solution)/shard_map/psum | solution.py:73
  333.3 0.6 broadcast_multiply_fusion.2
  333.9 0.0 copy-done.3
  333.9 1.0 convolution_bitcast_fusion.1
  334.9 0.0 copy-done.1
  334.9 7.3 fusion.4
  342.1 6.6 copy.24
  348.7 0.0 copy-start.4
  348.7 5.1 multiply_convert_fusion
  353.8 134.4 %reduce-scatter.5.cloned.1.call-done = bf16[512,256]{1,0:T(8,128)(2,1)} async-done(((bf16[16384,256]{1,0:T(8,128)(2,1)}), bf16[512,256]{1,0:T(8,128)(2,1)}) %reduce-scatter.5.cloned.1.call-update) | async-done | bytes 262160 | tf_op jit(solution)/shard_map/reduce_scatter | solution.py:62
  488.2 2.0 convolution_bitcast_fusion.2
  490.2 0.0 all-reduce.3.cloned.1.call-update
  490.2 0.0 copy-done.4
  490.2 1.2 fusion.14
  491.4 1.0 fusion.13
  492.4 256.2 %all-reduce.3.cloned.1.call-done = (f32[256,256]{0,1:T(8,128)}, f32[256,256]{0,1:T(8,128)}) async-done(((f32[256,256]{0,1:T(8,128)}, f32[256,256]{0,1:T(8,128)}), (f32[256,256]{0,1:T(8,128)}, f32[256,256]{0,1:T(8,128)})) %all-reduce.3.cloned.1.call-update) | async-done | bytes 524304 | tf_op jit(solution)/shard_map/psum | solution.py:73
  748.6 1.1 broadcast_multiply_fusion
  749.7 0.8 copy.26
  750.5 0.8 copy.25
  (3 shorter events, 0.0 us)
Async XLA Ops:
  7.2 1.0 copy-start
  7.2 104.8 %all-gather.3.cloned.1.call-start = ((), (), s32[]{:S(2)}) async-start(), calls=%async_computation.2 | async-start | bytes 8650752 | tf_op jit(solution)/shard_map/all_gather | solution.py:25
  10.0 147.5 %reduce-scatter.3.cloned.1.call-start = ((), (), s32[]{:S(2)}) async-start(), calls=%async_computation.3 | async-start | bytes 2359296 | tf_op jit(solution)/shard_map/reduce_scatter | solution.py:43
  112.0 9.5 %copy-start.2 = (bf16[1,1,96,128,128]{4,3,2,1,0:T(8,128)(2,1)S(1)}, bf16[1,1,96,128,128]{4,3,2,1,0:T(8,128)(2,1)}, u32[]{:S(2)}) copy-start(bf16[1,1,96,128,128]{4,3,2,1,0:T(8,128)(2,1)} %param.16) | copy-start | bytes 9437188
  121.5 36.0 %copy-start.5 = (bf16[256,256]{1,0:T(8,128)(2,1)S(1)}, bf16[256,256]{1,0:T(8,128)(2,1)}, u32[]{:S(2)}) copy-start(bf16[256,256]{1,0:T(8,128)(2,1)} %param.11) | copy-start | bytes 393220
  127.0 61.6 %all-gather.5.cloned.1.call-start = ((), (), s32[]{:S(2)}) async-start(), calls=%async_computation.4 | async-start | bytes 2359296 | tf_op jit(solution)/shard_map/all_gather | solution.py:48
  159.8 328.4 %reduce-scatter.5.cloned.1.call-start = ((), (), s32[]{:S(2)}) async-start(), calls=%async_computation.5 | async-start | bytes 8650752 | tf_op jit(solution)/shard_map/reduce_scatter | solution.py:62
  209.2 7.9 %copy-start.6 = (s32[1,1,96]{2,1,0:T(1,128)S(1)}, s32[1,1,96]{2,1,0:T(1,128)}, u32[]{:S(2)}) copy-start(s32[1,1,96]{2,1,0:T(1,128)} %param.14) | copy-start | bytes 1156
  255.1 78.7 %copy-start.3 = (bf16[512,256]{1,0:T(8,128)(2,1)S(1)}, bf16[512,256]{1,0:T(8,128)(2,1)}, u32[]{:S(2)}) copy-start(bf16[512,256]{1,0:T(8,128)(2,1)} %get-tuple-element.21) | copy-start | bytes 786436
  255.1 79.7 %copy-start.1 = (bf16[4096,256]{1,0:T(8,128)(2,1)S(1)}, bf16[4096,256]{1,0:T(8,128)(2,1)}, u32[]{:S(2)}) copy-start(bf16[4096,256]{1,0:T(8,128)(2,1)} %all-gather.5.cloned.1.call-done) | copy-start | bytes 6291460
  255.2 493.4 %all-reduce.3.cloned.1.call-start = ((), (), s32[]{:S(2)}) async-start(), calls=%async_computation.6 | async-start | bytes 1048576 | tf_op jit(solution)/shard_map/psum | solution.py:73
  348.7 141.5 %copy-start.4 = (bf16[256,256]{1,0:T(8,128)(2,1)S(1)}, bf16[256,256]{1,0:T(8,128)(2,1)}, u32[]{:S(2)}) copy-start(bf16[256,256]{1,0:T(8,128)(2,1)} %param.10) | copy-start | bytes 393220
Sparse Core Ops, SparseCore 0:
  11.1 100.8 all-gather.2
  127.1 30.3 reduce-scatter.2
  159.9 28.6 all-gather.4
  255.3 232.8 reduce-scatter.4
  494.2 254.3 all-reduce.2
where the time goes:
time: 758 us
  waiting for transfers between devices  550 us (73%)
  blocking collectives  78.1 us (10%)
  other arithmetic  46.2 us (6%)
  local copies, waits for them, and re-layouts  38.4 us (5%)
  matrix products  30 us (4%)
  between operations  14.5 us (2%)
    psum x1, waiting for transfers between devices, per_device(): lax.psum((local_msg, local_self, local_bias), ('row', 'col'))  256 us
    reduce_scatter x1, waiting for transfers between devices, per_device(): lax.psum_scatter(back_part.astype(jnp.bfloat16), 'row', scatter_dimension...  134 us
    all_gather x1, waiting for transfers between devices, per_device(): column_msgs = lax.all_gather(messages, 'row', axis=0, tiled=True)  101 us
    psum x1, blocking collectives, per_device(): lax.psum((local_msg, local_self, local_bias), ('row', 'col'))  78.1 us
    reduce_scatter x1, waiting for transfers between devices, per_device(): lax.psum_scatter(partial_value.astype(jnp.bfloat16), 'col', scatter_dimen...  30.4 us
    scatter-add x1, other arithmetic, per_device(): jax.ops.segment_sum(backward, slot_cols, num_segments=tile_cols)  29.1 us
    all_gather x1, waiting for transfers between devices, per_device(): grad_rows_all = lax.all_gather(grad_pre, 'col', axis=0, tiled=True)  28.7 us
  transfers between devices with their start and end apart: 5, of which 5 were waited for; matrix products, arithmetic and copies ran while one was open for 3% of the time, Pallas kernels for 0%

commit v1 on v0

--- a/solution.py
+++ b/solution.py
@@ -3,6 +3,13 @@
 import jax.numpy as jnp
 from jax import lax
 from jax.sharding import PartitionSpec as P
+
+
+def swapped_in(value, name, along):
+    count = lax.axis_size(name)
+    blocks = jnp.stack([value for _ in range(count)])
+    blocks = lax.all_to_all(blocks, name, split_axis=0, concat_axis=0)
+    return jnp.concatenate(blocks, axis=along)
 
 
 def activate(pre, row_mask, grad_in):
@@ -22,7 +29,7 @@
     messages = (jnp.dot(feats, w_msg, preferred_element_type=jnp.float32) * row_mask).astype(
         jnp.bfloat16
     )
-    column_msgs = lax.all_gather(messages, "row", axis=0, tiled=True)
+    column_msgs = swapped_in(messages, "row", 0)
     slot_cols = block_cols[0, 0]
     edge_block = edge_vals[0, 0]
     slot_total = edge_block.shape[0]

time: 758 us -> 869 us (1.15)
  waiting for transfers between devices: 550 us -> 647 us
  starting transfers between devices: 0.21 us -> 11.9 us
    all_to_all x0 -> x1, waiting for transfers between devices: none -> 188 us  [swapped_in(): blocks = lax.all_to_all(blocks, name, split_axis=0, concat_axis=0)]
    all_gather x1 -> x0, waiting for transfers between devices: 101 us -> none  [per_device(): column_msgs = lax.all_gather(messages, 'row', axis=0, tiled=True)]
    all_to_all x0 -> x1, starting transfers between devices: none -> 11.7 us  [swapped_in(): blocks = lax.all_to_all(blocks, name, split_axis=0, concat_axis=0)]
    reduce_scatter x1, waiting for transfers between devices: 30.4 us -> 39.5 us  [per_device(): lax.psum_scatter(partial_value.astype(jnp.bfloat16), 'col', scatter_dimen...]
where the time goes in v1:
time: 869 us; the launch traced here: 868 us
  waiting for transfers between devices  647 us (74%)
  blocking collectives  77.9 us (9%)
  other arithmetic  45.6 us (5%)
  local copies, waits for them, and re-layouts  42.6 us (5%)
  matrix products  29.3 us (3%)
  between operations  14.5 us (2%)
  starting transfers between devices  11.9 us (1%)
    psum x1, waiting for transfers between devices, per_device(): lax.psum((local_msg, local_self, local_bias), ('row', 'col'))  256 us
    all_to_all x1, waiting for transfers between devices, swapped_in(): blocks = lax.all_to_all(blocks, name, split_axis=0, concat_axis=0)  188 us
    reduce_scatter x1, waiting for transfers between devices, per_device(): lax.psum_scatter(back_part.astype(jnp.bfloat16), 'row', scatter_dimension...  135 us
    psum x1, blocking collectives, per_device(): lax.psum((local_msg, local_self, local_bias), ('row', 'col'))  77.9 us
    reduce_scatter x1, waiting for transfers between devices, per_device(): lax.psum_scatter(partial_value.astype(jnp.bfloat16), 'col', scatter_dimen...  39.5 us
    scatter-add x1, other arithmetic, per_device(): jax.ops.segment_sum(backward, slot_cols, num_segments=tile_cols)  29.1 us
    all_gather x1, waiting for transfers between devices, per_device(): grad_rows_all = lax.all_gather(grad_pre, 'col', axis=0, tiled=True)  28.8 us
  transfers between devices with their start and end apart: 5, of which 5 were waited for; matrix products, arithmetic and copies ran while one was open for 3% of the time, Pallas kernels for 0%

profile of v1, /device:TPU:2, one launch (start us, length us, event | category | flops | bytes accessed | tf_op | source)
XLA Modules:
  0.0 868.4 jit_solution(7515058434217326650)
XLA Ops:
  7.2 0.0 copy-start
  7.2 0.7 convert_element_type.67
  7.9 0.2 copy-done
  8.1 1.1 fusion.12
  9.3 4.2 stack.2
  13.5 0.0 copy-start.6
  13.5 11.7 %all-to-all-start = ((bf16[32,512,256]{2,1,0:T(8,128)(2,1)}), bf16[32,512,256]{2,1,0:T(8,128)(2,1)}, u32[]{:S(2)}, u32[]{:S(2)}) async-start(bf16[32,512,256]{2,1,0:T(8,128)(2,1)} %stack.2), calls=%async_computation | async-start | bytes 16777216 | tf_op jit(solution)/shard_map/all_to_all | solution.py:11
  25.2 0.0 reduce-scatter.3.cloned.1.call-start
  25.9 0.0 copy-done.6
  26.0 187.6 %all-to-all-done = bf16[32,512,256]{2,1,0:T(8,128)(2,1)} async-done(((bf16[32,512,256]{2,1,0:T(8,128)(2,1)}), bf16[32,512,256]{2,1,0:T(8,128)(2,1)}, u32[]{:S(2)}, u32[]{:S(2)}) %all-to-all-start) | async-done | bytes 8388640 | tf_op jit(solution)/shard_map/all_to_all | solution.py:11
  213.6 0.0 copy-start.2
  213.6 9.5 %gather_fusion = bf16[96,128,256]{2,1,0:T(8,128)(2,1)} fusion(bf16[128,128,256]{2,1,0:T(8,128)(2,1)} %bitcast.2, s32[1024]{0:T(1024)S(1)} %pad_clamp_fusion), kind=kCustom, calls=%fused_computation | custom fusion | bytes 12583296 | tf_op jit(solution)/shard_map/gather | solution.py:44
  223.1 0.0 copy-done.2
  223.1 0.0 copy-start.5
  223.1 5.5 bitcast_convert_fusion
  228.6 0.0 reduce-scatter.3.cloned.1.call-update
  228.6 0.0 all-gather.2.cloned.1.call-start
  228.6 39.5 %reduce-scatter.3.cloned.1.call-done = bf16[512,256]{1,0:T(8,128)(2,1)} async-done(((bf16[4096,256]{1,0:T(8,128)(2,1)}), bf16[512,256]{1,0:T(8,128)(2,1)}) %reduce-scatter.3.cloned.1.call-update) | async-done | bytes 262160 | tf_op jit(solution)/shard_map/reduce_scatter | solution.py:50
  268.1 0.0 copy-done.5
  268.1 2.3 convert_reduce_fusion
  270.4 0.0 all-gather.2.cloned.1.call-update
  270.5 0.0 reduce-scatter.5.cloned.1.call-start
  270.5 28.8 %all-gather.2.cloned.1.call-done = bf16[4096,256]{1,0:T(8,128)(2,1)} async-done(((bf16[512,256]{1,0:T(8,128)(2,1)}), bf16[4096,256]{1,0:T(8,128)(2,1)}) %all-gather.2.cloned.1.call-update) | async-done | bytes 2097168 | tf_op jit(solution)/shard_map/all_gather | solution.py:55
  299.4 8.0 convolution_bitcast_fusion
  307.3 12.6 %copy.22 = f32[3,32,128,256]{3,2,1,0:T(8,128)} copy(f32[3,32,128,256]{2,3,0,1:T(8,128)} %convolution_bitcast_fusion) | data formatting | bytes 25165824 | tf_op jit(solution)/shard_map/krij,rif->krjf/transpose | solution.py:57
  320.0 0.0 copy-start.7
  320.0 7.8 broadcast_in_dim.2
  327.8 0.0 copy-done.7
  327.8 29.1 %scatter_fusion = f32[128,128,256]{2,1,0:T(8,128)} fusion(f32[128,128,256]{2,1,0:T(8,128)} %broadcast_in_dim.2, s32[96]{0:T(128)S(1)} %bitcast.56, f32[96,128,256]{2,1,0:T(8,128)} %bitcast.46), kind=kCustom, calls=%fused_computation.1 | custom fusion | flops 3145728 | bytes 37749120 | tf_op jit(solution)/shard_map/scatter-add | solution.py:60
  356.9 9.0 %convert_element_type.75 = bf16[128,128,256]{2,1,0:T(8,128)(2,1)} convert(f32[128,128,256]{2,1,0:T(8,128)} %scatter_fusion) | non-fusion elementwise | flops 4194304 | bytes 25165824 | tf_op jit(solution)/shard_map/convert_element_type | solution.py:70
  365.9 0.0 copy-start.3
  365.9 0.0 copy-start.1
  365.9 0.0 reduce-scatter.5.cloned.1.call-update
  365.9 0.0 all-reduce.3.cloned.1.call-start
  366.0 77.9 %psum.23 = f32[256]{0:T(256)S(1)} all-reduce(f32[256]{0:T(256)S(1)} %get-tuple-element.20), channel_id=1, replica_groups=mesh['row'=32,'col'=8] {'row','col'}, use_global_device_ids=true, to_apply=%region_6.0 | all-reduce | flops 256 | bytes 2048 | tf_op jit(solution)/shard_map/psum | solution.py:80
  443.9 0.6 broadcast_multiply_fusion.2
  444.5 0.0 copy-done.3
  444.5 1.0 convolution_bitcast_fusion.1
  445.4 0.0 copy-done.1
  445.4 7.3 fusion.4
  452.7 6.6 copy.24
  459.3 0.0 copy-start.4
  459.3 5.1 multiply_convert_fusion
  464.4 134.5 %reduce-scatter.5.cloned.1.call-done = bf16[512,256]{1,0:T(8,128)(2,1)} async-done(((bf16[16384,256]{1,0:T(8,128)(2,1)}), bf16[512,256]{1,0:T(8,128)(2,1)}) %reduce-scatter.5.cloned.1.call-update) | async-done | bytes 262160 | tf_op jit(solution)/shard_map/reduce_scatter | solution.py:69
  598.9 2.0 convolution_bitcast_fusion.2
  600.9 0.0 all-reduce.3.cloned.1.call-update
  600.9 0.0 copy-done.4
  601.0 1.2 fusion.14
  602.2 1.0 fusion.13
  603.1 255.9 %all-reduce.3.cloned.1.call-done = (f32[256,256]{0,1:T(8,128)}, f32[256,256]{0,1:T(8,128)}) async-done(((f32[256,256]{0,1:T(8,128)}, f32[256,256]{0,1:T(8,128)}), (f32[256,256]{0,1:T(8,128)}, f32[256,256]{0,1:T(8,128)})) %all-reduce.3.cloned.1.call-update) | async-done | bytes 524304 | tf_op jit(solution)/shard_map/psum | solution.py:80
  859.1 1.1 broadcast_multiply_fusion
  860.2 0.8 copy.26
  861.0 0.8 copy.25
  (4 shorter events, 0.0 us)
Async XLA Ops:
  7.2 1.0 copy-start
  13.5 12.5 %copy-start.6 = (s32[1,1,96]{2,1,0:T(1,128)S(1)}, s32[1,1,96]{2,1,0:T(1,128)}, u32[]{:S(2)}) copy-start(s32[1,1,96]{2,1,0:T(1,128)} %param.14) | copy-start | bytes 1156
  13.5 200.1 %all-to-all-start = ((bf16[32,512,256]{2,1,0:T(8,128)(2,1)}), bf16[32,512,256]{2,1,0:T(8,128)(2,1)}, u32[]{:S(2)}, u32[]{:S(2)}) async-start(bf16[32,512,256]{2,1,0:T(8,128)(2,1)} %stack.2), calls=%async_computation | async-start | bytes 16777216 | tf_op jit(solution)/shard_map/all_to_all | solution.py:11
  25.2 242.9 %reduce-scatter.3.cloned.1.call-start = ((), (), s32[]{:S(2)}) async-start(), calls=%async_computation.3 | async-start | bytes 2359296 | tf_op jit(solution)/shard_map/reduce_scatter | solution.py:50
  213.6 9.5 %copy-start.2 = (bf16[1,1,96,128,128]{4,3,2,1,0:T(8,128)(2,1)S(1)}, bf16[1,1,96,128,128]{4,3,2,1,0:T(8,128)(2,1)}, u32[]{:S(2)}) copy-start(bf16[1,1,96,128,128]{4,3,2,1,0:T(8,128)(2,1)} %param.16) | copy-start | bytes 9437188
  223.1 45.1 %copy-start.5 = (bf16[256,256]{1,0:T(8,128)(2,1)S(1)}, bf16[256,256]{1,0:T(8,128)(2,1)}, u32[]{:S(2)}) copy-start(bf16[256,256]{1,0:T(8,128)(2,1)} %param.11) | copy-start | bytes 393220
  228.6 70.8 %all-gather.2.cloned.1.call-start = ((), (), s32[]{:S(2)}) async-start(), calls=%async_computation.4 | async-start | bytes 2359296 | tf_op jit(solution)/shard_map/all_gather | solution.py:55
  270.5 328.4 %reduce-scatter.5.cloned.1.call-start = ((), (), s32[]{:S(2)}) async-start(), calls=%async_computation.5 | async-start | bytes 8650752 | tf_op jit(solution)/shard_map/reduce_scatter | solution.py:69
  320.0 7.9 copy-start.7
  365.9 78.6 %copy-start.3 = (bf16[512,256]{1,0:T(8,128)(2,1)S(1)}, bf16[512,256]{1,0:T(8,128)(2,1)}, u32[]{:S(2)}) copy-start(bf16[512,256]{1,0:T(8,128)(2,1)} %get-tuple-element.21) | copy-start | bytes 786436
  365.9 79.5 %copy-start.1 = (bf16[4096,256]{1,0:T(8,128)(2,1)S(1)}, bf16[4096,256]{1,0:T(8,128)(2,1)}, u32[]{:S(2)}) copy-start(bf16[4096,256]{1,0:T(8,128)(2,1)} %all-gather.2.cloned.1.call-done) | copy-start | bytes 6291460
  365.9 493.2 %all-reduce.3.cloned.1.call-start = ((), (), s32[]{:S(2)}) async-start(), calls=%async_computation.6 | async-start | bytes 1048576 | tf_op jit(solution)/shard_map/psum | solution.py:80
  459.3 141.7 %copy-start.4 = (bf16[256,256]{1,0:T(8,128)(2,1)S(1)}, bf16[256,256]{1,0:T(8,128)(2,1)}, u32[]{:S(2)}) copy-start(bf16[256,256]{1,0:T(8,128)(2,1)} %param.10) | copy-start | bytes 393220
Sparse Core Ops, SparseCore 0:
  228.7 39.4 reduce-scatter.2
  270.6 28.7 all-gather.1
  366.1 232.8 reduce-scatter.4
  605.0 254.0 all-reduce.2
